TPU v7x, 256 devices: a whole 4x4x8 slice. The times are simulated.
256 devices in a mesh: dp: 4 (over y), space: 64 (over z, x, core).
Axes of the slice: x: 4, y: 4, z: 8, core: 2. Of those that a mesh axis runs over, the one named last changes fastest.
Arguments:
- features: bfloat16 [4, 128, 8, 8, 8, 128], P('dp', 'space'), may hold values from -6 to 6
- occupancy: int32 [4, 128, 8, 8, 8], P('dp', 'space'), may hold values from 0 to 1
- neighbours: int32 [4, 128, 26], P('dp', 'space'), may hold values from -1 to 127, as said below
- weight: bfloat16 [27, 128, 128], replicated, may hold values from -0.109375 to 0.109375
- cotangent: bfloat16 [4, 128, 8, 8, 8, 128], P('dp', 'space'), may hold values from -6 to 6
Outputs:
- response: bfloat16 [4, 128, 8, 8, 8, 128], P('dp', 'space')
- grad_input: bfloat16 [4, 128, 8, 8, 8, 128], P('dp', 'space')
- grad_weight: float32 [3456, 128], P('space')
Inputs may be any that keep to these rules, and one draw needn't show every extreme that they name: `neighbours`: A scan's blocks sit in a coarse grid of 64 slabs along the first dimension, each one cell thick and 4 cells across; each slab holds exactly 2 blocks, numbered slab by slab and inside a slab in the Morton order of their cells, so block g lies in slab g // 2; entry o of block g names the block in the adjacent cell in direction o, or -1 if that cell is empty or outside the grid; the relation is symmetric.
All inputs are finite; a program needn't handle non-finite values.
Results may differ from a plain program's by a relative error of at most 0.001.
Values may be sent and summed in bfloat16 or wider, within the bound.
A program may use at most 64 MiB of HBM per device.

v0:
```python
import math

import jax
import jax.numpy as jnp
from jax import lax
from jax.sharding import PartitionSpec as P

directions = [
    (along_x, along_y, along_z)
    for along_x in (-1, 0, 1)
    for along_y in (-1, 0, 1)
    for along_z in (-1, 0, 1)
    if (along_x, along_y, along_z) != (0, 0, 0)
]
kernel_taps = [
    (along_x, along_y, along_z)
    for along_x in range(3)
    for along_y in range(3)
    for along_z in range(3)
]


def padded_2(block, sides, width):
    for axis, dim in sides:
        count = lax.axis_size(axis)
        forward = [(i, i + 1) for i in range(count - 1)]
        backward = [(target, source) for source, target in forward]
        low = lax.ppermute(
            lax.slice_in_dim(block, block.shape[dim] - width, None, axis=dim), axis, forward
        )
        high = lax.ppermute(lax.slice_in_dim(block, 0, width, axis=dim), axis, backward)
        block = jnp.concatenate([low, block, high], axis=dim)
    return block


def side_slices(offset, extent):
    chosen = []
    for stride in offset:
        if stride == 1:
            chosen.append(slice(extent - 1, extent))
        elif stride == -1:
            chosen.append(slice(0, 1))
        else:
            chosen.append(slice(0, extent))
    return tuple(chosen)


def rim_slices(offset, extent):
    chosen = []
    for stride in offset:
        if stride == 1:
            chosen.append(slice(extent + 1, extent + 2))
        elif stride == -1:
            chosen.append(slice(0, 1))
        else:
            chosen.append(slice(1, extent + 1))
    return tuple(chosen)


def end_planes(field):
    count = field.shape[0]
    extent = field.shape[1]
    return jnp.stack([field[:, 0], field[:, extent - 1]]).reshape(2, count, -1)


def fill_rims(field, arrived, links, position):
    count = field.shape[0]
    extent = field.shape[1]
    channels = field.shape[-1]
    zero_bf = jnp.zeros((), jnp.bfloat16)
    before = arrived[0].reshape(count, extent, extent, channels)
    after = arrived[3].reshape(count, extent, extent, channels)
    padded = jnp.pad(field, ((0, 0), (1, 1), (1, 1), (1, 1), (0, 0)))
    whole = (slice(None),)
    for slot_index, offset in enumerate(directions):
        opposite = tuple((-stride for stride in offset))
        if offset[0] == 0:
            source = field[whole + side_slices(opposite, extent)]
        elif offset[0] == -1:
            source = before[whole + side_slices(opposite[1:], extent)][:, None]
        else:
            source = after[whole + side_slices(opposite[1:], extent)][:, None]
        other = links[:, slot_index]
        local = other - (position + offset[0]) * count
        picked = jnp.take(source, jnp.clip(local, 0, count - 1), axis=0)
        picked = jnp.where((other >= 0)[:, None, None, None, None], picked, zero_bf)
        padded = padded.at[whole + rim_slices(offset, extent)].set(picked)
    return padded


def window_at(padded, start_x, start_y, start_z, extent, block_lo, block_hi):
    channels = padded.shape[-1]
    return padded[
        block_lo:block_hi,
        start_x : start_x + extent,
        start_y : start_y + extent,
        start_z : start_z + extent,
    ].reshape(-1, channels)


def forward_each(padded_x, flat_g, weight, extent):
    count = padded_x.shape[0]
    channels = padded_x.shape[-1]
    summed = jnp.zeros((count * extent**3, channels), jnp.float32)
    grads = []
    for number, (along_x, along_y, along_z) in enumerate(kernel_taps):
        window = window_at(padded_x, along_x, along_y, along_z, extent, 0, count)
        summed = summed + jnp.dot(window, weight[number], preferred_element_type=jnp.float32)
        grads.append(
            lax.dot_general(
                window, flat_g, (((0,), (0,)), ((), ())), preferred_element_type=jnp.float32
            )
        )
    return (summed, jnp.concatenate(grads, axis=0))


def backward_each(padded_g, weight, extent):
    count = padded_g.shape[0]
    channels = padded_g.shape[-1]
    summed = jnp.zeros((count * extent**3, channels), jnp.float32)
    for number, (along_x, along_y, along_z) in enumerate(kernel_taps):
        window = window_at(padded_g, 2 - along_x, 2 - along_y, 2 - along_z, extent, 0, count)
        summed = summed + lax.dot_general(
            window, weight[number], (((1,), (1,)), ((), ())), preferred_element_type=jnp.float32
        )
    return summed


def per_device(features, occupancy, neighbours, weight, cotangent):
    count = features.shape[1]
    extent = features.shape[2]
    channels = features.shape[-1]
    devices = lax.axis_size("space")
    scans_count = lax.axis_size("dp")
    position = lax.axis_index("space")
    zero_bf = jnp.zeros((), jnp.bfloat16)
    zero_f = jnp.zeros((), jnp.float32)
    active = occupancy[0][..., None] > 0
    masked = jnp.where(active, features[0], zero_bf)
    upstream = jnp.where(active, cotangent[0], zero_bf)
    links = neighbours[0]
    arrived_x = padded_2(end_planes(masked), (("space", 0),), 1)
    padded_x = fill_rims(masked, arrived_x, links, position)
    flat_g = upstream.reshape(-1, channels)
    forward_sum, kernel_grad = forward_each(padded_x, flat_g, weight, extent)
    response = jnp.where(
        active, forward_sum.reshape(count, extent, extent, extent, channels), zero_f
    ).astype(jnp.bfloat16)
    arrived_g = padded_2(end_planes(upstream), (("space", 0),), 1)
    padded_g = fill_rims(upstream, arrived_g, links, position)
    backward_sum = backward_each(padded_g, weight, extent)
    grad_input = jnp.where(
        active, backward_sum.reshape(count, extent, extent, extent, channels), zero_f
    ).astype(jnp.bfloat16)
    across_scans = lax.psum(kernel_grad, "dp")
    shard_rows = lax.psum_scatter(across_scans, "space", scatter_dimension=0, tiled=True)
    scale_factor = 1.0 / math.sqrt(scans_count * devices * count * extent**3)
    return (response[None], grad_input[None], shard_rows * scale_factor)


def solution(mesh):
    placed = (
        P("dp", "space", None, None, None, None),
        P("dp", "space", None, None, None),
        P("dp", "space", None),
        P(),
        P("dp", "space", None, None, None, None),
    )
    return jax.shard_map(
        per_device,
        mesh=mesh,
        in_specs=placed,
        out_specs=(
            P("dp", "space", None, None, None, None),
            P("dp", "space", None, None, None, None),
            P("space", None),
        ),
        check_vma=False,
    )
```

profile of v0, /device:TPU:6, one launch (start us, length us, event | category | flops | bytes accessed | tf_op | source)
XLA Modules:
  0.0 260.6 jit_solution(3344975392172040905)
XLA Ops:
  1.5 1.2 bitcast_select_fusion
  2.8 1.9 collective-permute-start
  4.7 3.8 %collective-permute-start.2 = (bf16[1,2,8192]{2,1,0:T(2,128)(2,1)S(1)}, bf16[1,2,8192]{2,1,0:T(2,128)(2,1)S(1)}, u32[]{:S(2)}, u32[]{:S(2)}) collective-permute-start(bf16[1,2,8192]{2,1,0:T(2,128)(2,1)S(1)} %slice.2775), channel_id=1, source_target_pairs={{0,1},{1,2},{2,3},{3,4},{4,5},{5,6},{6,7},{7,8},{8,9},{9,10},{10,1... | collective-permute-start | bytes 98312 | tf_op jit(solution)/shard_map/ppermute | solution.py:28
  8.6 1.9 collective-permute-start.3
  10.5 2.2 collective-permute-start.1
  12.8 1.2 compare_reduce_fusion.19
  14.0 1.9 compare_reduce_fusion
  61.0 1.4 scatter.194
  62.4 1.4 scatter.195
  71.6 0.9 fusion.26
  72.5 0.9 fusion.25
  74.3 0.9 fusion.23
  75.2 0.9 fusion.22
  77.9 0.9 fusion.19
  79.7 0.9 fusion.17
  80.6 0.9 fusion.16
  82.4 0.9 fusion.14
  83.3 0.9 fusion.13
  84.2 0.9 fusion.12
  85.2 0.9 fusion.11
  86.1 0.9 fusion.10
  87.9 0.9 fusion.8
  90.6 0.9 fusion.5
  91.5 0.9 fusion.4
  93.3 0.9 fusion.2
  95.1 64.4 %fusion = f32[64,128]{1,0:T(8,128)S(1)} fusion(f32[3456,128]{1,0:T(8,128)} %fusion.1), kind=kCustom, calls=%all-reduce-scatter | all-reduce-scatter fusion | flops 524289 | bytes 1803264
  160.1 1.9 collective-permute-start.10
  162.0 4.2 %collective-permute-start.11 = (f32[64,128]{1,0:T(8,128)S(1)}, f32[64,128]{1,0:T(8,128)}, u32[]{:S(2)}, u32[]{:S(2)}) collective-permute-start(f32[64,128]{1,0:T(8,128)S(1)} %fusion), channel_id=1, source_target_pairs={{0,8},{1,9},{2,10},{3,11},{4,12},{5,13},{6,14},{7,15},{8,16},{9,17... | collective-permute-start | bytes 98312
  166.2 3.0 %collective-permute-start.12 = (f32[64,128]{1,0:T(8,128)S(1)}, f32[64,128]{1,0:T(8,128)}, u32[]{:S(2)}, u32[]{:S(2)}) collective-permute-start(f32[64,128]{1,0:T(8,128)S(1)} %fusion), channel_id=1, source_target_pairs={{0,9},{1,10},{2,11},{3,12},{4,13},{5,14},{6,15},{7,16},{8,17},{9,1... | collective-permute-start | bytes 98312
  169.2 3.3 %collective-permute-start.4 = (f32[64,128]{1,0:T(8,128)S(1)}, f32[64,128]{1,0:T(8,128)}, u32[]{:S(2)}, u32[]{:S(2)}) collective-permute-start(f32[64,128]{1,0:T(8,128)S(1)} %fusion), channel_id=1, source_target_pairs={{0,1},{1,2},{2,3},{3,4},{4,5},{5,6},{6,7},{7,8},{8,9},{9,10},{10,1... | collective-permute-start | bytes 98312
  172.5 1.4 fusion.184
  173.9 2.3 fusion.183
  179.1 0.9 scatter.224
  184.6 2.0 scatter.236
  186.7 2.0 scatter.239
  189.5 0.9 scatter.241
  194.1 0.9 scatter.251
  198.3 1.0 fusion.181
  199.3 3.9 %collective-permute-start.13 = (f32[54,128]{1,0:T(8,128)S(1)}, f32[54,128]{1,0:T(8,128)S(1)}, u32[]{:S(2)}, u32[]{:S(2)}) collective-permute-start(f32[54,128]{1,0:T(8,128)S(1)} %copy-done.22), channel_id=1, source_target_pairs={{0,10},{1,11},{2,12},{3,13},{4,14},{5,15},{6,16},{7,17},{8,18},{9,... | collective-permute-start | bytes 82952
  217.4 3.4 %collective-permute-start.5 = (f32[64,128]{1,0:T(8,128)S(1)}, f32[64,128]{1,0:T(8,128)S(1)}, u32[]{:S(2)}, u32[]{:S(2)}) collective-permute-start(f32[64,128]{1,0:T(8,128)S(1)} %fusion), channel_id=1, source_target_pairs={{0,2},{1,3},{2,4},{3,5},{4,6},{5,7},{6,8},{7,9},{8,10},{9,11},{10,... | collective-permute-start | bytes 98312
  220.9 2.6 collective-permute-start.6
  223.4 4.2 %collective-permute-start.7 = (f32[64,128]{1,0:T(8,128)S(1)}, f32[64,128]{1,0:T(8,128)S(1)}, u32[]{:S(2)}, u32[]{:S(2)}) collective-permute-start(f32[64,128]{1,0:T(8,128)S(1)} %fusion), channel_id=1, source_target_pairs={{0,4},{1,5},{2,6},{3,7},{4,8},{5,9},{6,10},{7,11},{8,12},{9,13},{1... | collective-permute-start | bytes 98312
  227.7 3.8 %collective-permute-start.8 = (f32[64,128]{1,0:T(8,128)S(1)}, f32[64,128]{1,0:T(8,128)S(1)}, u32[]{:S(2)}, u32[]{:S(2)}) collective-permute-start(f32[64,128]{1,0:T(8,128)S(1)} %fusion), channel_id=1, source_target_pairs={{0,5},{1,6},{2,7},{3,8},{4,9},{5,10},{6,11},{7,12},{8,13},{9,14},{... | collective-permute-start | bytes 98312
  231.5 1.9 collective-permute-start.9
  233.5 1.0 select_convert_fusion
  234.5 4.0 %collective-permute-done.9 = f32[64,128]{1,0:T(8,128)S(1)} collective-permute-done((f32[64,128]{1,0:T(8,128)S(1)}, f32[64,128]{1,0:T(8,128)S(1)}, u32[]{:S(2)}, u32[]{:S(2)}) %collective-permute-start.9) | collective-permute-done | bytes 32800
  238.6 4.2 %concatenate.156 = f32[694,128]{1,0:T(8,128)S(1)} concatenate(f32[54,128]{1,0:T(8,128)S(1)} %collective-permute-done.13, f32[64,128]{1,0:T(8,128)} %collective-permute-done.12, f32[64,128]{1,0:T(8,128)} %collective-permute-done.11, f32[64,128]{1,0:T(8,128)} %collective-permute-done.10, f32[64,128]{1,0:T(8,128)S(1)} %collective-permute-done.9, ...), dimensions={0} | concatenate | bytes 710656
  242.8 17.2 %psum.8 = f32[54,128]{1,0:T(8,128)S(1)} all-reduce(f32[54,128]{1,0:T(8,128)S(1)} %constant_dynamic-slice_fusion), channel_id=1, replica_groups=mesh['dp'=4,'space'=64] {'dp'}, use_global_device_ids=true, to_apply=%region_0.8 | all-reduce | flops 6912 | bytes 55296 | tf_op jit(solution)/shard_map/psum | solution.py:155
  (364 shorter events, 91.6 us)
Async XLA Ops:
  0.6 15.6 %copy-start.1 = (s32[1,2,26]{2,1,0:T(2,128)S(1)}, s32[1,2,26]{2,1,0:T(2,128)}, u32[]{:S(2)}) copy-start(s32[1,2,26]{2,1,0:T(2,128)} %param.125) | copy-start | bytes 628
  2.8 30.8 %collective-permute-start = (bf16[1,2,8192]{2,1,0:T(2,128)(2,1)S(1)}, bf16[1,2,8192]{2,1,0:T(2,128)(2,1)S(1)}, u32[]{:S(2)}, u32[]{:S(2)}) collective-permute-start(bf16[1,2,8192]{2,1,0:T(2,128)(2,1)S(1)} %slice.2668), channel_id=1, source_target_pairs={{0,1},{1,2},{2,3},{3,4},{4,5},{5,6},{6,7},{7,8},{8,9},{9,10},{10,1... | collective-permute-start | bytes 98312 | tf_op jit(solution)/shard_map/ppermute | solution.py:28
  4.7 28.8 %collective-permute-start.2 = (bf16[1,2,8192]{2,1,0:T(2,128)(2,1)S(1)}, bf16[1,2,8192]{2,1,0:T(2,128)(2,1)S(1)}, u32[]{:S(2)}, u32[]{:S(2)}) collective-permute-start(bf16[1,2,8192]{2,1,0:T(2,128)(2,1)S(1)} %slice.2775), channel_id=1, source_target_pairs={{0,1},{1,2},{2,3},{3,4},{4,5},{5,6},{6,7},{7,8},{8,9},{9,10},{10,1... | collective-permute-start | bytes 98312 | tf_op jit(solution)/shard_map/ppermute | solution.py:28
  8.6 25.1 %collective-permute-start.3 = (bf16[1,2,8192]{2,1,0:T(2,128)(2,1)S(1)}, bf16[1,2,8192]{2,1,0:T(2,128)(2,1)S(1)}, u32[]{:S(2)}, u32[]{:S(2)}) collective-permute-start(bf16[1,2,8192]{2,1,0:T(2,128)(2,1)S(1)} %slice.2793), channel_id=1, source_target_pairs={{1,0},{2,1},{3,2},{4,3},{5,4},{6,5},{7,6},{8,7},{9,8},{10,9},{11,1... | collective-permute-start | bytes 98312 | tf_op jit(solution)/shard_map/ppermute | solution.py:31
  10.5 23.1 %collective-permute-start.1 = (bf16[1,2,8192]{2,1,0:T(2,128)(2,1)S(1)}, bf16[1,2,8192]{2,1,0:T(2,128)(2,1)S(1)}, u32[]{:S(2)}, u32[]{:S(2)}) collective-permute-start(bf16[1,2,8192]{2,1,0:T(2,128)(2,1)S(1)} %slice.2703), channel_id=1, source_target_pairs={{1,0},{2,1},{3,2},{4,3},{5,4},{6,5},{7,6},{8,7},{9,8},{10,9},{11,1... | collective-permute-start | bytes 98312 | tf_op jit(solution)/shard_map/ppermute | solution.py:31
  22.2 10.1 %copy-start.23 = (u32[256]{0:T(256)S(1)}, u32[256]{0:T(256)}, u32[]{:S(2)}) copy-start(u32[256]{0:T(256)} %constant.1500) | copy-start | bytes 3076
  160.1 60.7 %collective-permute-start.10 = (f32[64,128]{1,0:T(8,128)S(1)}, f32[64,128]{1,0:T(8,128)}, u32[]{:S(2)}, u32[]{:S(2)}) collective-permute-start(f32[64,128]{1,0:T(8,128)S(1)} %fusion), channel_id=1, source_target_pairs={{0,7},{1,8},{2,9},{3,10},{4,11},{5,12},{6,13},{7,14},{8,15},{9,16}... | collective-permute-start | bytes 98312
  162.0 61.4 %collective-permute-start.11 = (f32[64,128]{1,0:T(8,128)S(1)}, f32[64,128]{1,0:T(8,128)}, u32[]{:S(2)}, u32[]{:S(2)}) collective-permute-start(f32[64,128]{1,0:T(8,128)S(1)} %fusion), channel_id=1, source_target_pairs={{0,8},{1,9},{2,10},{3,11},{4,12},{5,13},{6,14},{7,15},{8,16},{9,17... | collective-permute-start | bytes 98312
  166.2 61.4 %collective-permute-start.12 = (f32[64,128]{1,0:T(8,128)S(1)}, f32[64,128]{1,0:T(8,128)}, u32[]{:S(2)}, u32[]{:S(2)}) collective-permute-start(f32[64,128]{1,0:T(8,128)S(1)} %fusion), channel_id=1, source_target_pairs={{0,9},{1,10},{2,11},{3,12},{4,13},{5,14},{6,15},{7,16},{8,17},{9,1... | collective-permute-start | bytes 98312
  169.2 62.3 %collective-permute-start.4 = (f32[64,128]{1,0:T(8,128)S(1)}, f32[64,128]{1,0:T(8,128)}, u32[]{:S(2)}, u32[]{:S(2)}) collective-permute-start(f32[64,128]{1,0:T(8,128)S(1)} %fusion), channel_id=1, source_target_pairs={{0,1},{1,2},{2,3},{3,4},{4,5},{5,6},{6,7},{7,8},{8,9},{9,10},{10,1... | collective-permute-start | bytes 98312
  198.3 1.0 copy-start.22
  198.3 4.9 %copy-start = (bf16[27,128,128]{2,1,0:T(8,128)(2,1)S(1)}, bf16[27,128,128]{2,1,0:T(8,128)(2,1)}, u32[]{:S(2)}) copy-start(bf16[27,128,128]{2,1,0:T(8,128)(2,1)} %param.126) | copy-start | bytes 2654212
  199.3 4.4 %copy-start.21 = (bf16[2,8,8,8,128]{4,3,2,1,0:T(8,128)(2,1)S(1)}, bf16[2,8,8,8,128]{4,3,2,1,0:T(8,128)(2,1)}, u32[]{:S(2)}) copy-start(bf16[2,8,8,8,128]{4,3,2,1,0:T(8,128)(2,1)} %get-tuple-element.738) | copy-start | bytes 786436
  199.3 4.6 %copy-start.20 = (bf16[2,8,8,8,128]{4,3,2,1,0:T(8,128)(2,1)S(1)}, bf16[2,8,8,8,128]{4,3,2,1,0:T(8,128)(2,1)}, u32[]{:S(2)}) copy-start(bf16[2,8,8,8,128]{4,3,2,1,0:T(8,128)(2,1)} %get-tuple-element.737) | copy-start | bytes 786436
  199.3 18.1 %collective-permute-start.13 = (f32[54,128]{1,0:T(8,128)S(1)}, f32[54,128]{1,0:T(8,128)S(1)}, u32[]{:S(2)}, u32[]{:S(2)}) collective-permute-start(f32[54,128]{1,0:T(8,128)S(1)} %copy-done.22), channel_id=1, source_target_pairs={{0,10},{1,11},{2,12},{3,13},{4,14},{5,15},{6,16},{7,17},{8,18},{9,... | collective-permute-start | bytes 82952
  203.4 1.0 copy-start.19
  203.7 1.0 copy-start.18
  203.9 1.0 copy-start.17
  204.4 1.0 copy-start.16
  204.6 1.0 copy-start.15
  204.9 1.0 copy-start.14
  205.4 1.0 copy-start.13
  205.6 1.0 copy-start.12
  205.9 1.0 copy-start.11
  206.4 1.0 copy-start.10
  206.6 1.0 copy-start.9
  206.9 1.0 copy-start.8
  207.3 1.0 copy-start.7
  207.6 1.0 copy-start.6
  207.9 1.0 copy-start.5
  208.3 1.0 copy-start.4
  208.6 1.0 copy-start.3
  208.9 1.0 copy-start.2
  217.4 17.0 %collective-permute-start.5 = (f32[64,128]{1,0:T(8,128)S(1)}, f32[64,128]{1,0:T(8,128)S(1)}, u32[]{:S(2)}, u32[]{:S(2)}) collective-permute-start(f32[64,128]{1,0:T(8,128)S(1)} %fusion), channel_id=1, source_target_pairs={{0,2},{1,3},{2,4},{3,5},{4,6},{5,7},{6,8},{7,9},{8,10},{9,11},{10,... | collective-permute-start | bytes 98312
  220.9 13.6 %collective-permute-start.6 = (f32[64,128]{1,0:T(8,128)S(1)}, f32[64,128]{1,0:T(8,128)S(1)}, u32[]{:S(2)}, u32[]{:S(2)}) collective-permute-start(f32[64,128]{1,0:T(8,128)S(1)} %fusion), channel_id=1, source_target_pairs={{0,3},{1,4},{2,5},{3,6},{4,7},{5,8},{6,9},{7,10},{8,11},{9,12},{10... | collective-permute-start | bytes 98312
  223.4 11.1 %collective-permute-start.7 = (f32[64,128]{1,0:T(8,128)S(1)}, f32[64,128]{1,0:T(8,128)S(1)}, u32[]{:S(2)}, u32[]{:S(2)}) collective-permute-start(f32[64,128]{1,0:T(8,128)S(1)} %fusion), channel_id=1, source_target_pairs={{0,4},{1,5},{2,6},{3,7},{4,8},{5,9},{6,10},{7,11},{8,12},{9,13},{1... | collective-permute-start | bytes 98312
  227.7 6.8 %collective-permute-start.8 = (f32[64,128]{1,0:T(8,128)S(1)}, f32[64,128]{1,0:T(8,128)S(1)}, u32[]{:S(2)}, u32[]{:S(2)}) collective-permute-start(f32[64,128]{1,0:T(8,128)S(1)} %fusion), channel_id=1, source_target_pairs={{0,5},{1,6},{2,7},{3,8},{4,9},{5,10},{6,11},{7,12},{8,13},{9,14},{... | collective-permute-start | bytes 98312
  231.5 7.0 %collective-permute-start.9 = (f32[64,128]{1,0:T(8,128)S(1)}, f32[64,128]{1,0:T(8,128)S(1)}, u32[]{:S(2)}, u32[]{:S(2)}) collective-permute-start(f32[64,128]{1,0:T(8,128)S(1)} %fusion), channel_id=1, source_target_pairs={{0,6},{1,7},{2,8},{3,9},{4,10},{5,11},{6,12},{7,13},{8,14},{9,15},... | collective-permute-start | bytes 98312
where the time goes:
time: 263 us; the launch traced here: 261 us
  blocking collectives  81.5 us (31%)
  local copies, waits for them, and re-layouts  68.6 us (26%)
  starting transfers between devices  42.1 us (16%)
  matrix products  36.2 us (14%)
  other arithmetic  25.1 us (10%)
  waiting for transfers between devices  4.08 us (2%)
  between operations  3 us (1%)
    unnamed x1, blocking collectives  64.4 us
    unnamed x10, starting transfers between devices  32.2 us
    gather x52, local copies, waits for them, and re-layouts, fill_rims(): picked = jnp.take(source, jnp.clip(local, 0, count - 1), axis=0)  29.1 us
    scatter x52, local copies, waits for them, and re-layouts, fill_rims(): padded = padded.at[whole + rim_slices(offset, extent)].set(picked)  25.9 us
    dot_general x27, matrix products, forward_each(): lax.dot_general(window, flat_g, (((0,), (0,)), ((), ())), preferred_eleme...  24.4 us
    psum x1, blocking collectives, per_device(): across_scans = lax.psum(kernel_grad, 'dp')  17.2 us
    select_n x26, other arithmetic, fill_rims(): picked = jnp.where((other >= 0)[:, None, None, None, None], picked, zero_bf)  17.2 us
    unnamed x68, local copies, waits for them, and re-layouts  7.65 us
  transfers between devices with their start and end apart: 14, of which 1 were waited for; matrix products, arithmetic and copies ran while one was open for 23% of the time, Pallas kernels for 0%

commit v1 on v0

v1 whole, which is shorter than its diff:
```python
import functools
import math

import jax
import jax.numpy as jnp
from jax import lax
from jax.experimental import pallas as pl
from jax.experimental.pallas import tpu as pltpu
from jax.sharding import PartitionSpec as P

MESH = pl.DeviceIdType.MESH
BF = jnp.bfloat16
F32 = jnp.float32
ROWS = 54
PART = 16
CHUNKS = ((3, 2), (0, 3), (5, 3))
TX_ORDER = (1, 0, 2)


def slot_of(dx, dy, dz):
    number = 9 * (dx + 1) + 3 * (dy + 1) + (dz + 1)
    return number if number < 13 else number - 1


def kernel(
    x_hbm, g_hbm, occ_hbm, links, w_hbm,
    resp_hbm, gin_hbm, gw_ref,
    xv, gv, occv, wv, wt, mask, xm, gm, gmb, gt, xs, gs,
    halo_out, halo_in, cbuf, csnd, crcv, xyb, own, rxy, zp, rz, fin, outv,
    in_sem, out_sem, halo_s, halo_r, core_s, core_r, xy_s, xy_r, z_s, z_r, y_s, y_r,
):
    me_y = lax.axis_index("dp")
    me_s = lax.axis_index("space")
    me_c = lax.rem(me_s, 2)
    me_x = lax.rem(me_s // 2, 4)
    me_z = me_s // 8
    other_c = 1 - me_c

    def at(y, z, x, c):
        return (y, (z * 4 + x) * 2 + c)

    after = (me_y, lax.rem(me_s + 1, 64))
    before = (me_y, lax.rem(me_s + 63, 64))
    partner = at(me_y, me_z, me_x, other_c)

    def xy_peer(k):
        return lax.rem(me_x + k // 4, 4), lax.rem(me_y + lax.rem(k, 4), 4)

    loads = [
        pltpu.make_async_copy(src, dst, in_sem.at[i])
        for i, (src, dst) in enumerate(
            ((occ_hbm, occv), (x_hbm, xv), (g_hbm, gv), (w_hbm, wv))
        )
    ]
    for load in loads:
        load.start()

    barrier = pltpu.get_barrier_semaphore()

    def greet(device):
        pl.semaphore_signal(barrier, inc=1, device_id=device, device_id_type=MESH)

    greet(before)
    greet(after)
    greet(partner)

    def greet_xy(k, carry):
        px, py = xy_peer(k)
        greet(at(py, me_z, px, me_c))
        return carry

    lax.fori_loop(1, 16, greet_xy, 0)

    def greet_z(k, carry):
        greet(at(me_y, lax.rem(me_z + k, 8), me_x, me_c))
        return carry

    lax.fori_loop(1, 8, greet_z, 0)

    for load in loads[:3]:
        load.wait()

    eye = (
        lax.broadcasted_iota(jnp.int32, (8, 8, 8), 1)
        == lax.broadcasted_iota(jnp.int32, (8, 8, 8), 2)
    )
    ones = jnp.ones((8, 128), F32)

    def mask_plane(i, carry):
        occ = occv[i // 8, lax.rem(i, 8)]
        spread = jnp.broadcast_to(occ[:, None, :], (8, 8, 8))
        picked = jnp.where(eye & (spread > 0), 1.0, 0.0).astype(F32).reshape(64, 8)
        m = jnp.dot(picked, ones, preferred_element_type=F32)
        mask[i] = m
        keep = m > 0.5
        xk = jnp.where(keep, xv[i].astype(F32), 0.0)
        gk = jnp.where(keep, gv[i].astype(F32), 0.0)
        xm[i] = xk.reshape(8, 8, 128)
        gm[i] = gk.reshape(8, 8, 128)
        gmb[i] = gk.astype(BF)
        return carry

    lax.fori_loop(0, 16, mask_plane, 0)

    for t, src in enumerate((xm, gm)):
        for side in range(2):
            for b in range(2):
                halo_out[t, side, b] = src[8 * b + 7 * side].reshape(64, 128).astype(BF)

    pl.semaphore_wait(barrier, 25)

    def halo_copy(t, side):
        return pltpu.make_async_remote_copy(
            src_ref=halo_out.at[t, side],
            dst_ref=halo_in.at[t, 1 - side],
            send_sem=halo_s.at[t, side],
            recv_sem=halo_r.at[t, 1 - side],
            device_id=after if side == 1 else before,
            device_id_type=MESH,
        )

    halos = [[halo_copy(t, side) for side in range(2)] for t in range(2)]
    for t in range(2):
        for side in range(2):
            halos[t][side].start()

    zi = lax.broadcasted_iota(jnp.int32, (10, 8, 128), 1)

    def weights_of(b, dx, local):
        wanted = (me_s + dx) * 2 + local

        def one(dy, dz):
            link = links[b, slot_of(dx, dy, dz)]
            return jnp.where((link == wanted) & (link >= 0), 1.0, 0.0).astype(F32)

        return one

    def put_plane(dst, index, centre, low, high):
        shifted = (
            pltpu.roll(jnp.where(zi == 7, low, centre), 1, 1),
            centre,
            pltpu.roll(jnp.where(zi == 0, high, centre), 7, 1),
        )
        for ty in range(3):
            for tz in range(3):
                col = (3 * ty + tz) * 128
                dst[index, :, col : col + 128] = (
                    shifted[tz][ty : ty + 8].reshape(64, 128).astype(BF)
                )

    def own_planes(src, dst):
        for b in range(2):
            one = weights_of(b, 0, 1 - b)
            w = {
                (dy, dz): one(dy, dz)
                for dy in (-1, 0, 1)
                for dz in (-1, 0, 1)
                if (dy, dz) != (0, 0)
            }

            def plane(p, carry, b=b, w=w):
                mine = src[8 * b + p]
                theirs = src[8 * (1 - b) + p]
                first, last = theirs[0:1], theirs[7:8]

                def zone(dz):
                    middle = mine if dz == 0 else theirs * w[0, dz]
                    return jnp.concatenate(
                        [last * w[-1, dz], middle, first * w[1, dz]], axis=0
                    )

                put_plane(dst, 10 * b + p + 1, zone(0), zone(-1), zone(1))
                return carry

            lax.fori_loop(0, 8, plane, 0)

    def rim_planes(t, dst):
        for side, dx in ((0, -1), (1, 1)):
            p0 = halo_in[t, side, 0].astype(F32).reshape(8, 8, 128)
            p1 = halo_in[t, side, 1].astype(F32).reshape(8, 8, 128)
            for b in range(2):
                w0 = weights_of(b, dx, 0)
                w1 = weights_of(b, dx, 1)

                def zone(dz):
                    def mix(dy, rows):
                        return p0[rows] * w0(dy, dz) + p1[rows] * w1(dy, dz)

                    return jnp.concatenate(
                        [mix(-1, slice(7, 8)), mix(0, slice(0, 8)), mix(1, slice(0, 1))],
                        axis=0,
                    )

                put_plane(dst, 10 * b + 9 * side, zone(0), zone(-1), zone(1))

    def kernel_grad(tx):
        for ty in range(3):
            total = None
            for b in range(2):
                window = xs[10 * b + tx : 10 * b + tx + 8, :, 384 * ty : 384 * ty + 384]
                part = jnp.dot(
                    gt[:, 512 * b : 512 * b + 512],
                    window.reshape(512, 384),
                    preferred_element_type=F32,
                )
                total = part if total is None else total + part
            for tz in range(3):
                tap = 9 * tx + 3 * ty + tz
                cbuf[128 * tap : 128 * tap + 128, :] = total[:, 128 * tz : 128 * tz + 128].T

    def core_copy(n):
        z0, nz = CHUNKS[n]
        return pltpu.make_async_remote_copy(
            src_ref=csnd.at[pl.ds(4 * z0, 4 * nz)],
            dst_ref=crcv.at[pl.ds(4 * z0, 4 * nz)],
            send_sem=core_s.at[n],
            recv_sem=core_r.at[n],
            device_id=partner,
            device_id_type=MESH,
        )

    def core_send(n):
        z0, nz = CHUNKS[n]

        def fill(j, carry):
            csnd[j] = cbuf[pl.ds(ROWS * (2 * j + other_c), 64), :]
            return carry

        lax.fori_loop(4 * z0, 4 * (z0 + nz), fill, 0)
        core_copy(n).start()

    def xy_copy(n, k):
        z0, nz = CHUNKS[n]
        px, py = xy_peer(k)
        return pltpu.make_async_remote_copy(
            src_ref=xyb.at[px, py, pl.ds(z0, nz)],
            dst_ref=rxy.at[k - 1, pl.ds(z0, nz)],
            send_sem=xy_s.at[n, k - 1],
            recv_sem=xy_r.at[n, k - 1],
            device_id=at(py, me_z, px, me_c),
            device_id_type=MESH,
        )

    def xy_send(n):
        z0, nz = CHUNKS[n]
        core_copy(n).wait()

        def fill(j, carry):
            summed = cbuf[pl.ds(ROWS * (2 * j + me_c), 64), :] + crcv[j]
            for q in range(4):
                xyb[lax.rem(j, 4), q, j // 4] = summed[PART * q : PART * q + PART]
            return carry

        lax.fori_loop(4 * z0, 4 * (z0 + nz), fill, 0)

        def go(k, carry):
            xy_copy(n, k).start()
            return carry

        lax.fori_loop(1, 16, go, 0)

        def keep(z, carry):
            j = 4 * z + me_x
            own[z] = (
                cbuf[pl.ds(ROWS * (2 * j + me_c) + PART * me_y, PART), :]
                + crcv[j, pl.ds(pl.multiple_of(PART * me_y, PART), PART), :]
            )
            return carry

        lax.fori_loop(z0, z0 + nz, keep, 0)

    def z_copy(slot, target):
        return pltpu.make_async_remote_copy(
            src_ref=zp.at[target],
            dst_ref=rz.at[slot],
            send_sem=z_s.at[target],
            recv_sem=z_r.at[slot],
            device_id=at(me_y, target, me_x, me_c),
            device_id_type=MESH,
        )

    def z_send(n):
        z0, nz = CHUNKS[n]

        def arrived(k, carry):
            xy_copy(n, k).wait()
            return carry

        lax.fori_loop(1, 16, arrived, 0)

        def add(z, carry):
            total = own[z]
            for k in range(15):
                total = total + rxy[k, z]
            zp[z] = total

            @pl.when(z != me_z)
            def _():
                z_copy(me_z, z).start()

            return carry

        lax.fori_loop(z0, z0 + nz, add, 0)

    def transposed_weights():
        def turn(t, carry):
            wt[26 - t] = wv[t].T
            return carry

        lax.fori_loop(0, 27, turn, 0)

    def product(shifts, taps, out_index, out_hbm, part):
        b = part // 2
        start = 10 * b + 4 * lax.rem(part, 2)
        total = None
        for tx in range(3):
            window = shifts[pl.ds(start + tx, 4)].reshape(256, 1152)
            piece = jnp.dot(
                window, taps[9 * tx : 9 * tx + 9].reshape(1152, 128),
                preferred_element_type=F32,
            )
            total = piece if total is None else total + piece
        planes = pl.ds(4 * part, 4)
        keep = mask[planes].reshape(256, 128) > 0.5
        outv[out_index, planes] = jnp.where(keep, total, 0.0).astype(BF).reshape(4, 64, 128)

    def products(shifts, taps, out_index, out_hbm, lo, hi):
        def one(part, carry):
            product(shifts, taps, out_index, out_hbm, part)
            return carry

        lax.fori_loop(lo, hi, one, 0)

    def out_copy(index):
        dst = (resp_hbm, gin_hbm)[index]
        return pltpu.make_async_copy(outv.at[index], dst, out_sem.at[index])

    own_planes(xm, xs)
    for k in range(8):
        gt[:, 128 * k : 128 * k + 128] = gmb[2 * k : 2 * k + 2].reshape(128, 128).T
    kernel_grad(1)
    core_send(0)
    halos[0][0].wait()
    halos[0][1].wait()
    rim_planes(0, xs)
    kernel_grad(0)
    core_send(1)
    xy_send(0)
    kernel_grad(2)
    core_send(2)
    xy_send(1)
    own_planes(gm, gs)
    xy_send(2)

    loads[3].wait()
    z_send(0)
    products(xs, wv, 0, resp_hbm, 0, 2)
    z_send(1)
    products(xs, wv, 0, resp_hbm, 2, 4)
    out_copy(0).start()
    z_send(2)
    halos[1][0].wait()
    halos[1][1].wait()
    rim_planes(1, gs)
    transposed_weights()
    products(gs, wt, 1, gin_hbm, 0, 2)

    def z_done(k, carry):
        source = lax.rem(me_z + k, 8)
        z_copy(source, source).wait_recv()
        z_copy(me_z, source).wait_send()
        return carry

    lax.fori_loop(1, 8, z_done, 0)
    rz[me_z] = zp[me_z]
    total = rz[0]
    for z in range(1, 8):
        total = total + rz[z]
    fin[me_y] = total * (1.0 / math.sqrt(4 * 128 * 8**3))

    def y_copy(slot, k):
        return pltpu.make_async_remote_copy(
            src_ref=fin.at[me_y],
            dst_ref=fin.at[slot],
            send_sem=y_s.at[k],
            recv_sem=y_r.at[slot],
            device_id=at(lax.rem(me_y + k, 4), me_z, me_x, me_c),
            device_id_type=MESH,
        )

    for k in range(1, 4):
        y_copy(me_y, k).start()
    products(gs, wt, 1, gin_hbm, 2, 4)
    out_copy(1).start()
    for k in range(1, 4):
        y_copy(lax.rem(me_y + k, 4), k).wait_recv()
        y_copy(me_y, k).wait_send()
    gw_ref[...] = fin[...].reshape(64, 128)[:ROWS]
    out_copy(0).wait()
    out_copy(1).wait()


def per_device(features, occupancy, neighbours, weight, cotangent):
    dma = pltpu.SemaphoreType.DMA
    anywhere = pl.BlockSpec(memory_space=pl.ANY)
    resp, gin, gw = pl.pallas_call(
        kernel,
        out_shape=(
            jax.ShapeDtypeStruct((16, 64, 128), BF),
            jax.ShapeDtypeStruct((16, 64, 128), BF),
            jax.ShapeDtypeStruct((ROWS, 128), F32),
        ),
        in_specs=[
            anywhere,
            anywhere,
            anywhere,
            pl.BlockSpec(memory_space=pltpu.SMEM),
            anywhere,
        ],
        out_specs=(anywhere, anywhere, pl.BlockSpec(memory_space=pltpu.VMEM)),
        scratch_shapes=[
            pltpu.VMEM((16, 64, 128), BF),
            pltpu.VMEM((16, 64, 128), BF),
            pltpu.VMEM((2, 8, 8, 8), jnp.int32),
            pltpu.VMEM((27, 128, 128), BF),
            pltpu.VMEM((27, 128, 128), BF),
            pltpu.VMEM((16, 64, 128), F32),
            pltpu.VMEM((16, 8, 8, 128), F32),
            pltpu.VMEM((16, 8, 8, 128), F32),
            pltpu.VMEM((16, 64, 128), BF),
            pltpu.VMEM((128, 1024), BF),
            pltpu.VMEM((20, 64, 1152), BF),
            pltpu.VMEM((20, 64, 1152), BF),
            pltpu.VMEM((2, 2, 2, 64, 128), BF),
            pltpu.VMEM((2, 2, 2, 64, 128), BF),
            pltpu.VMEM((3472, 128), F32),
            pltpu.VMEM((32, 64, 128), F32),
            pltpu.VMEM((32, 64, 128), F32),
            pltpu.VMEM((4, 4, 8, PART, 128), F32),
            pltpu.VMEM((8, PART, 128), F32),
            pltpu.VMEM((15, 8, PART, 128), F32),
            pltpu.VMEM((8, PART, 128), F32),
            pltpu.VMEM((8, PART, 128), F32),
            pltpu.VMEM((4, PART, 128), F32),
            pltpu.VMEM((2, 16, 64, 128), BF),
            dma((4,)),
            dma((2,)),
            dma((2, 2)),
            dma((2, 2)),
            dma((3,)),
            dma((3,)),
            dma((3, 15)),
            dma((3, 15)),
            dma((8,)),
            dma((8,)),
            dma((4,)),
            dma((4,)),
        ],
        compiler_params=pltpu.CompilerParams(collective_id=0, has_side_effects=True),
        name="sparse_conv_step",
    )(
        features.reshape(16, 64, 128),
        cotangent.reshape(16, 64, 128),
        occupancy[0],
        neighbours[0],
        weight,
    )
    shape = features.shape
    return resp.reshape(shape), gin.reshape(shape), gw


def solution(mesh):
    placed = (
        P("dp", "space", None, None, None, None),
        P("dp", "space", None, None, None),
        P("dp", "space", None),
        P(),
        P("dp", "space", None, None, None, None),
    )
    return jax.shard_map(
        per_device,
        mesh=mesh,
        in_specs=placed,
        out_specs=(
            P("dp", "space", None, None, None, None),
            P("dp", "space", None, None, None, None),
            P("space", None),
        ),
        check_vma=False,
    )
```

time: 263 us -> 41.7 us (0.16)
  the two profiles are of different devices: /device:TPU:6 before, /device:TPU:1 now
where the time goes in v1:
time: 41.7 us; the launch traced here: 41.5 us
  Pallas kernels  37.8 us (91%)
  local copies, waits for them, and re-layouts  3.07 us (7%)
  between operations  0.65 us (2%)
    pallas_call x1, Pallas kernels, per_device(): pl.pallas_call(kernel, out_shape=(jax.ShapeDtypeStruct((16, 64, 128), BF)...  37.8 us
    unnamed x7, local copies, waits for them, and re-layouts  3.07 us

profile of v1, /device:TPU:1, one launch (start us, length us, event | category | flops | bytes accessed | tf_op | source)
XLA Modules:
  0.0 41.5 jit_solution(2597376479837730232)
XLA Ops:
  0.6 37.8 %sparse_conv_step.1 = (bf16[16,64,128]{2,1,0:T(8,128)(2,1)}, bf16[16,64,128]{2,1,0:T(8,128)(2,1)}, f32[54,128]{1,0:T(8,128)}) custom-call(bf16[16,64,128]{2,1,0:T(8,128)(2,1)} %bitcast.6, bf16[16,64,128]{2,1,0:T(8,128)(2,1)} %bitcast.7, s32[2,8,8,8]{3,2,1,0:T(8,128)} %bitcast.10, s32[2,26]{1,0:T(2,128)} %bitcast.11, bf16[27,128,128]{2,1,0:T(8,128)(2,1)} %w_hbm.1), custom_call_target="tpu_custom_call" | custom-call | tf_op jit(solution)/shard_map/sparse_conv_step/pallas_call | solution.py:406
  38.4 0.0 copy-start
  38.4 1.7 %copy.11 = bf16[1,2,8,8,8,128]{5,4,3,2,1,0:T(8,128)(2,1)} copy(bf16[1,2,8,8,8,128]{5,4,3,2,1,0:T(8,128)(2,1)} %bitcast.9) | data formatting | bytes 524288
  40.2 0.0 copy-done
  40.2 0.0 copy-start.1
  40.2 0.7 %copy.12 = bf16[1,2,8,8,8,128]{5,4,3,2,1,0:T(8,128)(2,1)} copy(bf16[1,2,8,8,8,128]{5,4,3,2,1,0:T(8,128)(2,1)S(1)} %bitcast.8) | data formatting | bytes 524288
  40.9 0.0 copy-done.1
  40.9 0.6 %copy.13 = f32[54,128]{1,0:T(8,128)} copy(f32[54,128]{1,0:T(8,128)S(1)} %copy-done.1) | data formatting | bytes 55296
Async XLA Ops:
  38.4 1.7 %copy-start = (bf16[16,64,128]{2,1,0:T(8,128)(2,1)S(1)}, bf16[16,64,128]{2,1,0:T(8,128)(2,1)}, u32[]{:S(2)}) copy-start(bf16[16,64,128]{2,1,0:T(8,128)(2,1)} %get-tuple-element.7) | copy-start | bytes 786436
  40.2 0.7 %copy-start.1 = (f32[54,128]{1,0:T(8,128)S(1)}, f32[54,128]{1,0:T(8,128)}, u32[]{:S(2)}) copy-start(f32[54,128]{1,0:T(8,128)} %get-tuple-element.14) | copy-start | bytes 82948

commit v2 on v1

--- a/solution.py
+++ b/solution.py
@@ -12,9 +12,9 @@
 BF = jnp.bfloat16
 F32 = jnp.float32
 ROWS = 54
-PART = 16
+PART = 14
+SLOT = 16
 CHUNKS = ((3, 2), (0, 3), (5, 3))
-TX_ORDER = (1, 0, 2)
 
 
 def slot_of(dx, dy, dz):
@@ -26,8 +26,8 @@
     x_hbm, g_hbm, occ_hbm, links, w_hbm,
     resp_hbm, gin_hbm, gw_ref,
     xv, gv, occv, wv, wt, mask, xm, gm, gmb, gt, xs, gs,
-    halo_out, halo_in, cbuf, csnd, crcv, xyb, own, rxy, zp, rz, fin, outv,
-    in_sem, out_sem, halo_s, halo_r, core_s, core_r, xy_s, xy_r, z_s, z_r, y_s, y_r,
+    halo_x, halo_g, halo_o, cbuf, csnd, crcv, xyb, own, rxy, zp, rz, fin, outv,
+    in_sem, out_sem, halo_s, halo_r, core_s, core_r, xy_s, xy_r, z_s, z_r, y_s, y_r, ready,
 ):
     me_y = lax.axis_index("dp")
     me_s = lax.axis_index("space")
@@ -60,22 +60,46 @@
     def greet(device):
         pl.semaphore_signal(barrier, inc=1, device_id=device, device_id_type=MESH)
 
-    greet(before)
-    greet(after)
-    greet(partner)
-
-    def greet_xy(k, carry):
-        px, py = xy_peer(k)
-        greet(at(py, me_z, px, me_c))
-        return carry
-
-    lax.fori_loop(1, 16, greet_xy, 0)
-
-    def greet_z(k, carry):
-        greet(at(me_y, lax.rem(me_z + k, 8), me_x, me_c))
-        return carry
-
-    lax.fori_loop(1, 8, greet_z, 0)
+    near = [
+        at(me_y, me_z, lax.rem(me_x + d, 4), me_c) for d in (1, 3)
+    ] + [
+        at(lax.rem(me_y + d, 4), me_z, me_x, me_c) for d in (1, 3)
+    ] + [
+        at(me_y, lax.rem(me_z + d, 8), me_x, me_c) for d in (1, 7)
+    ]
+    for device in [before, after, partner] + near:
+        greet(device)
+
+    def round_signal(r):
+        for device in near:
+            pl.semaphore_signal(ready.at[r], inc=1, device_id=device, device_id_type=MESH)
+
+    def round_wait(r):
+        pl.semaphore_wait(ready.at[r], 6)
+
+    pl.semaphore_wait(barrier, 9)
+
+    def halo_copies(side):
+        plane = 7 * side
+        return [
+            pltpu.make_async_remote_copy(
+                src_ref=src.at[:, plane],
+                dst_ref=dst.at[1 - side],
+                send_sem=halo_s.at[t, side],
+                recv_sem=halo_r.at[t, 1 - side],
+                device_id=after if side == 1 else before,
+                device_id_type=MESH,
+            )
+            for t, (src, dst) in enumerate(
+                ((occ_hbm, halo_o), (x_hbm, halo_x), (g_hbm, halo_g))
+            )
+        ]
+
+    halos = [halo_copies(0), halo_copies(1)]
+    for t in range(3):
+        for side in range(2):
+            halos[side][t].start()
+    round_signal(0)
 
     for load in loads[:3]:
         load.wait()
@@ -86,43 +110,24 @@
     )
     ones = jnp.ones((8, 128), F32)
 
-    def mask_plane(i, carry):
-        occ = occv[i // 8, lax.rem(i, 8)]
+    def mask_of(occ):
         spread = jnp.broadcast_to(occ[:, None, :], (8, 8, 8))
         picked = jnp.where(eye & (spread > 0), 1.0, 0.0).astype(F32).reshape(64, 8)
-        m = jnp.dot(picked, ones, preferred_element_type=F32)
+        return jnp.dot(picked, ones, preferred_element_type=F32)
+
+    def mask_plane(i, carry):
+        b, p = i // 8, lax.rem(i, 8)
+        m = mask_of(occv[b, p])
         mask[i] = m
         keep = m > 0.5
-        xk = jnp.where(keep, xv[i].astype(F32), 0.0)
-        gk = jnp.where(keep, gv[i].astype(F32), 0.0)
+        xk = jnp.where(keep, xv[b, p].astype(F32), 0.0)
+        gk = jnp.where(keep, gv[b, p].astype(F32), 0.0)
         xm[i] = xk.reshape(8, 8, 128)
         gm[i] = gk.reshape(8, 8, 128)
         gmb[i] = gk.astype(BF)
         return carry
 
-    lax.fori_loop(0, 16, mask_plane, 0)
-
-    for t, src in enumerate((xm, gm)):
-        for side in range(2):
-            for b in range(2):
-                halo_out[t, side, b] = src[8 * b + 7 * side].reshape(64, 128).astype(BF)
-
-    pl.semaphore_wait(barrier, 25)
-
-    def halo_copy(t, side):
-        return pltpu.make_async_remote_copy(
-            src_ref=halo_out.at[t, side],
-            dst_ref=halo_in.at[t, 1 - side],
-            send_sem=halo_s.at[t, side],
-            recv_sem=halo_r.at[t, 1 - side],
-            device_id=after if side == 1 else before,
-            device_id_type=MESH,
-        )
-
-    halos = [[halo_copy(t, side) for side in range(2)] for t in range(2)]
-    for t in range(2):
-        for side in range(2):
-            halos[t][side].start()
+    lax.fori_loop(0, 16, mask_plane, 0, unroll=4)
 
     zi = lax.broadcasted_iota(jnp.int32, (10, 8, 128), 1)
 
@@ -174,10 +179,14 @@
 
             lax.fori_loop(0, 8, plane, 0)
 
-    def rim_planes(t, dst):
+    def rim_planes(halo, dst):
         for side, dx in ((0, -1), (1, 1)):
-            p0 = halo_in[t, side, 0].astype(F32).reshape(8, 8, 128)
-            p1 = halo_in[t, side, 1].astype(F32).reshape(8, 8, 128)
+            p0, p1 = (
+                jnp.where(
+                    mask_of(halo_o[side, b]) > 0.5, halo[side, b].astype(F32), 0.0
+                ).reshape(8, 8, 128)
+                for b in range(2)
+            )
             for b in range(2):
                 w0 = weights_of(b, dx, 0)
                 w1 = weights_of(b, dx, 1)
@@ -223,7 +232,8 @@
         z0, nz = CHUNKS[n]
 
         def fill(j, carry):
-            csnd[j] = cbuf[pl.ds(ROWS * (2 * j + other_c), 64), :]
+            for q in range(4):
+                csnd[j, q] = cbuf[pl.ds(ROWS * (2 * j + other_c) + PART * q, SLOT), :]
             return carry
 
         lax.fori_loop(4 * z0, 4 * (z0 + nz), fill, 0)
@@ -246,9 +256,9 @@
         core_copy(n).wait()
 
         def fill(j, carry):
-            summed = cbuf[pl.ds(ROWS * (2 * j + me_c), 64), :] + crcv[j]
             for q in range(4):
-                xyb[lax.rem(j, 4), q, j // 4] = summed[PART * q : PART * q + PART]
+                mine = cbuf[pl.ds(ROWS * (2 * j + me_c) + PART * q, SLOT), :]
+                xyb[lax.rem(j, 4), q, j // 4] = mine + crcv[j, q]
             return carry
 
         lax.fori_loop(4 * z0, 4 * (z0 + nz), fill, 0)
@@ -262,8 +272,8 @@
         def keep(z, carry):
             j = 4 * z + me_x
             own[z] = (
-                cbuf[pl.ds(ROWS * (2 * j + me_c) + PART * me_y, PART), :]
-                + crcv[j, pl.ds(pl.multiple_of(PART * me_y, PART), PART), :]
+                cbuf[pl.ds(ROWS * (2 * j + me_c) + PART * me_y, SLOT), :]
+                + crcv[j, me_y]
             )
             return carry
 
@@ -335,19 +345,26 @@
         dst = (resp_hbm, gin_hbm)[index]
         return pltpu.make_async_copy(outv.at[index], dst, out_sem.at[index])
 
+    cbuf[128 * 27 :, :] = jnp.zeros((SLOT, 128), F32)
     own_planes(xm, xs)
     for k in range(8):
         gt[:, 128 * k : 128 * k + 128] = gmb[2 * k : 2 * k + 2].reshape(128, 128).T
     kernel_grad(1)
     core_send(0)
-    halos[0][0].wait()
-    halos[0][1].wait()
-    rim_planes(0, xs)
+    round_wait(0)
+    round_signal(1)
+    for side in range(2):
+        halos[side][0].wait()
+        halos[side][1].wait()
+    rim_planes(halo_x, xs)
     kernel_grad(0)
     core_send(1)
-    xy_send(0)
+    round_wait(1)
+    round_signal(2)
     kernel_grad(2)
     core_send(2)
+    round_wait(2)
+    xy_send(0)
     xy_send(1)
     own_planes(gm, gs)
     xy_send(2)
@@ -359,9 +376,9 @@
     products(xs, wv, 0, resp_hbm, 2, 4)
     out_copy(0).start()
     z_send(2)
-    halos[1][0].wait()
-    halos[1][1].wait()
-    rim_planes(1, gs)
+    halos[0][2].wait()
+    halos[1][2].wait()
+    rim_planes(halo_g, gs)
     transposed_weights()
     products(gs, wt, 1, gin_hbm, 0, 2)
 
@@ -395,7 +412,9 @@
     for k in range(1, 4):
         y_copy(lax.rem(me_y + k, 4), k).wait_recv()
         y_copy(me_y, k).wait_send()
-    gw_ref[...] = fin[...].reshape(64, 128)[:ROWS]
+    for q in range(4):
+        rows = min(PART, ROWS - PART * q)
+        gw_ref[PART * q : PART * q + rows, :] = fin[q, :rows]
     out_copy(0).wait()
     out_copy(1).wait()
 
@@ -419,8 +438,8 @@
         ],
         out_specs=(anywhere, anywhere, pl.BlockSpec(memory_space=pltpu.VMEM)),
         scratch_shapes=[
-            pltpu.VMEM((16, 64, 128), BF),
-            pltpu.VMEM((16, 64, 128), BF),
+            pltpu.VMEM((2, 8, 64, 128), BF),
+            pltpu.VMEM((2, 8, 64, 128), BF),
             pltpu.VMEM((2, 8, 8, 8), jnp.int32),
             pltpu.VMEM((27, 128, 128), BF),
             pltpu.VMEM((27, 128, 128), BF),
@@ -431,22 +450,23 @@
             pltpu.VMEM((128, 1024), BF),
             pltpu.VMEM((20, 64, 1152), BF),
             pltpu.VMEM((20, 64, 1152), BF),
-            pltpu.VMEM((2, 2, 2, 64, 128), BF),
-            pltpu.VMEM((2, 2, 2, 64, 128), BF),
+            pltpu.VMEM((2, 2, 64, 128), BF),
+            pltpu.VMEM((2, 2, 64, 128), BF),
+            pltpu.VMEM((2, 2, 8, 8), jnp.int32),
             pltpu.VMEM((3472, 128), F32),
-            pltpu.VMEM((32, 64, 128), F32),
-            pltpu.VMEM((32, 64, 128), F32),
-            pltpu.VMEM((4, 4, 8, PART, 128), F32),
-            pltpu.VMEM((8, PART, 128), F32),
-            pltpu.VMEM((15, 8, PART, 128), F32),
-            pltpu.VMEM((8, PART, 128), F32),
-            pltpu.VMEM((8, PART, 128), F32),
-            pltpu.VMEM((4, PART, 128), F32),
+            pltpu.VMEM((32, 4, SLOT, 128), F32),
+            pltpu.VMEM((32, 4, SLOT, 128), F32),
+            pltpu.VMEM((4, 4, 8, SLOT, 128), F32),
+            pltpu.VMEM((8, SLOT, 128), F32),
+            pltpu.VMEM((15, 8, SLOT, 128), F32),
+            pltpu.VMEM((8, SLOT, 128), F32),
+            pltpu.VMEM((8, SLOT, 128), F32),
+            pltpu.VMEM((4, SLOT, 128), F32),
             pltpu.VMEM((2, 16, 64, 128), BF),
             dma((4,)),
             dma((2,)),
-            dma((2, 2)),
-            dma((2, 2)),
+            dma((3, 2)),
+            dma((3, 2)),
             dma((3,)),
             dma((3,)),
             dma((3, 15)),
@@ -455,12 +475,13 @@
             dma((8,)),
             dma((4,)),
             dma((4,)),
+            pltpu.SemaphoreType.REGULAR((3,)),
         ],
         compiler_params=pltpu.CompilerParams(collective_id=0, has_side_effects=True),
         name="sparse_conv_step",
     )(
-        features.reshape(16, 64, 128),
-        cotangent.reshape(16, 64, 128),
+        features.reshape(2, 8, 64, 128),
+        cotangent.reshape(2, 8, 64, 128),
         occupancy[0],
         neighbours[0],
         weight,

time: 41.7 us -> 43.5 us (1.043)
  Pallas kernels: 37.8 us -> 39.6 us
    pallas_call x1, Pallas kernels: 37.8 us -> 39.6 us  [per_device(): pl.pallas_call(kernel, out_shape=(jax.ShapeDtypeStruct((16, 64, 128), BF)...]
where the time goes in v2:
time: 43.5 us; the launch traced here: 43.3 us
  Pallas kernels  39.6 us (91%)
  local copies, waits for them, and re-layouts  3.07 us (7%)
  between operations  0.65 us (1%)
    pallas_call x1, Pallas kernels, per_device(): pl.pallas_call(kernel, out_shape=(jax.ShapeDtypeStruct((16, 64, 128), BF)...  39.6 us
    unnamed x7, local copies, waits for them, and re-layouts  3.07 us

profile of v2, /device:TPU:1, one launch (start us, length us, event | category | flops | bytes accessed | tf_op | source)
XLA Modules:
  0.0 43.3 jit_solution(9865616858309190853)
XLA Ops:
  0.6 39.6 %sparse_conv_step.1 = (bf16[16,64,128]{2,1,0:T(8,128)(2,1)}, bf16[16,64,128]{2,1,0:T(8,128)(2,1)}, f32[54,128]{1,0:T(8,128)}) custom-call(bf16[2,8,64,128]{3,2,1,0:T(8,128)(2,1)} %bitcast.6, bf16[2,8,64,128]{3,2,1,0:T(8,128)(2,1)} %bitcast.7, s32[2,8,8,8]{3,2,1,0:T(8,128)} %bitcast.10, s32[2,26]{1,0:T(2,128)} %bitcast.11, bf16[27,128,128]{2,1,0:T(8,128)(2,1)} %w_hbm.1), custom_call_target="tpu_custom_call" | custom-call | tf_op jit(solution)/shard_map/sparse_conv_step/pallas_call | solution.py:425
  40.2 0.0 copy-start
  40.2 1.7 %copy.11 = bf16[1,2,8,8,8,128]{5,4,3,2,1,0:T(8,128)(2,1)} copy(bf16[1,2,8,8,8,128]{5,4,3,2,1,0:T(8,128)(2,1)} %bitcast.9) | data formatting | bytes 524288
  41.9 0.0 copy-done
  41.9 0.0 copy-start.1
  41.9 0.7 %copy.12 = bf16[1,2,8,8,8,128]{5,4,3,2,1,0:T(8,128)(2,1)} copy(bf16[1,2,8,8,8,128]{5,4,3,2,1,0:T(8,128)(2,1)S(1)} %bitcast.8) | data formatting | bytes 524288
  42.7 0.0 copy-done.1
  42.7 0.6 %copy.13 = f32[54,128]{1,0:T(8,128)} copy(f32[54,128]{1,0:T(8,128)S(1)} %copy-done.1) | data formatting | bytes 55296
Async XLA Ops:
  40.2 1.7 %copy-start = (bf16[16,64,128]{2,1,0:T(8,128)(2,1)S(1)}, bf16[16,64,128]{2,1,0:T(8,128)(2,1)}, u32[]{:S(2)}) copy-start(bf16[16,64,128]{2,1,0:T(8,128)(2,1)} %get-tuple-element.7) | copy-start | bytes 786436
  41.9 0.7 %copy-start.1 = (f32[54,128]{1,0:T(8,128)S(1)}, f32[54,128]{1,0:T(8,128)}, u32[]{:S(2)}) copy-start(f32[54,128]{1,0:T(8,128)} %get-tuple-element.14) | copy-start | bytes 82948

commit v3 on v2

--- a/solution.py
+++ b/solution.py
@@ -239,6 +239,21 @@
         lax.fori_loop(4 * z0, 4 * (z0 + nz), fill, 0)
         core_copy(n).start()
 
+    row_of = lax.broadcasted_iota(jnp.int32, (SLOT, 128), 0)
+
+    def coded(v):
+        top = jnp.max(jnp.abs(v), axis=0, keepdims=True)
+        power = jnp.ceil(jnp.log2(jnp.maximum(top, 2e-33) * (1.0 / 32000.0)))
+        return (
+            jnp.where(row_of == PART, power, jnp.round(v * jnp.exp2(-power)))
+            .astype(jnp.int32)
+            .astype(jnp.int16)
+        )
+
+    def decoded(c):
+        v = c.astype(jnp.int32).astype(F32)
+        return v * jnp.exp2(v[PART : PART + 1])
+
     def xy_copy(n, k):
         z0, nz = CHUNKS[n]
         px, py = xy_peer(k)
@@ -258,7 +273,7 @@
         def fill(j, carry):
             for q in range(4):
                 mine = cbuf[pl.ds(ROWS * (2 * j + me_c) + PART * q, SLOT), :]
-                xyb[lax.rem(j, 4), q, j // 4] = mine + crcv[j, q]
+                xyb[lax.rem(j, 4), q, j // 4] = coded(mine + crcv[j, q])
             return carry
 
         lax.fori_loop(4 * z0, 4 * (z0 + nz), fill, 0)
@@ -301,7 +316,7 @@
         def add(z, carry):
             total = own[z]
             for k in range(15):
-                total = total + rxy[k, z]
+                total = total + decoded(rxy[k, z])
             zp[z] = total
 
             @pl.when(z != me_z)
@@ -366,21 +381,20 @@
     round_wait(2)
     xy_send(0)
     xy_send(1)
+    loads[3].wait()
+    products(xs, wv, 0, resp_hbm, 0, 1)
+    xy_send(2)
     own_planes(gm, gs)
-    xy_send(2)
-
-    loads[3].wait()
-    z_send(0)
-    products(xs, wv, 0, resp_hbm, 0, 2)
-    z_send(1)
-    products(xs, wv, 0, resp_hbm, 2, 4)
-    out_copy(0).start()
-    z_send(2)
     halos[0][2].wait()
     halos[1][2].wait()
     rim_planes(halo_g, gs)
     transposed_weights()
-    products(gs, wt, 1, gin_hbm, 0, 2)
+    products(xs, wv, 0, resp_hbm, 1, 4)
+    out_copy(0).start()
+    z_send(0)
+    z_send(1)
+    z_send(2)
+    products(gs, wt, 1, gin_hbm, 0, 3)
 
     def z_done(k, carry):
         source = lax.rem(me_z + k, 8)
@@ -407,7 +421,7 @@
 
     for k in range(1, 4):
         y_copy(me_y, k).start()
-    products(gs, wt, 1, gin_hbm, 2, 4)
+    products(gs, wt, 1, gin_hbm, 3, 4)
     out_copy(1).start()
     for k in range(1, 4):
         y_copy(lax.rem(me_y + k, 4), k).wait_recv()
@@ -456,9 +470,9 @@
             pltpu.VMEM((3472, 128), F32),
             pltpu.VMEM((32, 4, SLOT, 128), F32),
             pltpu.VMEM((32, 4, SLOT, 128), F32),
-            pltpu.VMEM((4, 4, 8, SLOT, 128), F32),
+            pltpu.VMEM((4, 4, 8, SLOT, 128), jnp.int16),
             pltpu.VMEM((8, SLOT, 128), F32),
-            pltpu.VMEM((15, 8, SLOT, 128), F32),
+            pltpu.VMEM((15, 8, SLOT, 128), jnp.int16),
             pltpu.VMEM((8, SLOT, 128), F32),
             pltpu.VMEM((8, SLOT, 128), F32),
             pltpu.VMEM((4, SLOT, 128), F32),

time: 43.5 us -> 36.6 us (0.84)
  Pallas kernels: 39.6 us -> 32.6 us
    pallas_call x1, Pallas kernels: 39.6 us -> 32.6 us  [per_device(): pl.pallas_call(kernel, out_shape=(jax.ShapeDtypeStruct((16, 64, 128), BF)...]
where the time goes in v3:
time: 36.6 us; the launch traced here: 36.4 us
  Pallas kernels  32.6 us (89%)
  local copies, waits for them, and re-layouts  3.07 us (8%)
  between operations  0.65 us (2%)
    pallas_call x1, Pallas kernels, per_device(): pl.pallas_call(kernel, out_shape=(jax.ShapeDtypeStruct((16, 64, 128), BF)...  32.6 us
    unnamed x7, local copies, waits for them, and re-layouts  3.07 us

profile of v3, /device:TPU:1, one launch (start us, length us, event | category | flops | bytes accessed | tf_op | source)
XLA Modules:
  0.0 36.4 jit_solution(16084289609637461600)
XLA Ops:
  0.6 32.6 %sparse_conv_step.1 = (bf16[16,64,128]{2,1,0:T(8,128)(2,1)}, bf16[16,64,128]{2,1,0:T(8,128)(2,1)}, f32[54,128]{1,0:T(8,128)}) custom-call(bf16[2,8,64,128]{3,2,1,0:T(8,128)(2,1)} %bitcast.6, bf16[2,8,64,128]{3,2,1,0:T(8,128)(2,1)} %bitcast.7, s32[2,8,8,8]{3,2,1,0:T(8,128)} %bitcast.10, s32[2,26]{1,0:T(2,128)} %bitcast.11, bf16[27,128,128]{2,1,0:T(8,128)(2,1)} %w_hbm.1), custom_call_target="tpu_custom_call" | custom-call | tf_op jit(solution)/shard_map/sparse_conv_step/pallas_call | solution.py:439
  33.3 0.0 copy-start
  33.3 1.7 %copy.11 = bf16[1,2,8,8,8,128]{5,4,3,2,1,0:T(8,128)(2,1)} copy(bf16[1,2,8,8,8,128]{5,4,3,2,1,0:T(8,128)(2,1)} %bitcast.9) | data formatting | bytes 524288
  35.0 0.0 copy-done
  35.0 0.0 copy-start.1
  35.0 0.7 %copy.12 = bf16[1,2,8,8,8,128]{5,4,3,2,1,0:T(8,128)(2,1)} copy(bf16[1,2,8,8,8,128]{5,4,3,2,1,0:T(8,128)(2,1)S(1)} %bitcast.8) | data formatting | bytes 524288
  35.7 0.0 copy-done.1
  35.8 0.6 %copy.13 = f32[54,128]{1,0:T(8,128)} copy(f32[54,128]{1,0:T(8,128)S(1)} %copy-done.1) | data formatting | bytes 55296
Async XLA Ops:
  33.3 1.7 %copy-start = (bf16[16,64,128]{2,1,0:T(8,128)(2,1)S(1)}, bf16[16,64,128]{2,1,0:T(8,128)(2,1)}, u32[]{:S(2)}) copy-start(bf16[16,64,128]{2,1,0:T(8,128)(2,1)} %get-tuple-element.7) | copy-start | bytes 786436
  35.0 0.7 %copy-start.1 = (f32[54,128]{1,0:T(8,128)S(1)}, f32[54,128]{1,0:T(8,128)}, u32[]{:S(2)}) copy-start(f32[54,128]{1,0:T(8,128)} %get-tuple-element.14) | copy-start | bytes 82948

commit v4 on v3

--- a/solution.py
+++ b/solution.py
@@ -24,10 +24,10 @@
 
 def kernel(
     x_hbm, g_hbm, occ_hbm, links, w_hbm,
-    resp_hbm, gin_hbm, gw_ref,
+    resp_ref, gin_ref, gw_ref,
     xv, gv, occv, wv, wt, mask, xm, gm, gmb, gt, xs, gs,
-    halo_x, halo_g, halo_o, cbuf, csnd, crcv, xyb, own, rxy, zp, rz, fin, outv,
-    in_sem, out_sem, halo_s, halo_r, core_s, core_r, xy_s, xy_r, z_s, z_r, y_s, y_r, ready,
+    halo_x, halo_g, halo_o, cbuf, csnd, crcv, xyb, own, rxy, zp, rz, fin,
+    in_sem, halo_s, halo_r, core_s, core_r, xy_s, xy_r, z_s, z_r, y_s, y_r, ready,
 ):
     me_y = lax.axis_index("dp")
     me_s = lax.axis_index("space")
@@ -236,7 +236,7 @@
                 csnd[j, q] = cbuf[pl.ds(ROWS * (2 * j + other_c) + PART * q, SLOT), :]
             return carry
 
-        lax.fori_loop(4 * z0, 4 * (z0 + nz), fill, 0)
+        lax.fori_loop(4 * z0, 4 * (z0 + nz), fill, 0, unroll=4)
         core_copy(n).start()
 
     row_of = lax.broadcasted_iota(jnp.int32, (SLOT, 128), 0)
@@ -276,7 +276,7 @@
                 xyb[lax.rem(j, 4), q, j // 4] = coded(mine + crcv[j, q])
             return carry
 
-        lax.fori_loop(4 * z0, 4 * (z0 + nz), fill, 0)
+        lax.fori_loop(4 * z0, 4 * (z0 + nz), fill, 0, unroll=4)
 
         def go(k, carry):
             xy_copy(n, k).start()
@@ -318,14 +318,18 @@
             for k in range(15):
                 total = total + decoded(rxy[k, z])
             zp[z] = total
-
+            return carry
+
+        lax.fori_loop(z0, z0 + nz, add, 0, unroll=True)
+
+        def send(z, carry):
             @pl.when(z != me_z)
             def _():
                 z_copy(me_z, z).start()
 
             return carry
 
-        lax.fori_loop(z0, z0 + nz, add, 0)
+        lax.fori_loop(z0, z0 + nz, send, 0)
 
     def transposed_weights():
         def turn(t, carry):
@@ -334,7 +338,7 @@
 
         lax.fori_loop(0, 27, turn, 0)
 
-    def product(shifts, taps, out_index, out_hbm, part):
+    def product(shifts, taps, out, part):
         b = part // 2
         start = 10 * b + 4 * lax.rem(part, 2)
         total = None
@@ -347,54 +351,50 @@
             total = piece if total is None else total + piece
         planes = pl.ds(4 * part, 4)
         keep = mask[planes].reshape(256, 128) > 0.5
-        outv[out_index, planes] = jnp.where(keep, total, 0.0).astype(BF).reshape(4, 64, 128)
-
-    def products(shifts, taps, out_index, out_hbm, lo, hi):
+        out[planes] = jnp.where(keep, total, 0.0).astype(BF).reshape(4, 64, 128)
+
+    def products(shifts, taps, out, lo, hi):
         def one(part, carry):
-            product(shifts, taps, out_index, out_hbm, part)
+            product(shifts, taps, out, part)
             return carry
 
         lax.fori_loop(lo, hi, one, 0)
 
-    def out_copy(index):
-        dst = (resp_hbm, gin_hbm)[index]
-        return pltpu.make_async_copy(outv.at[index], dst, out_sem.at[index])
-
     cbuf[128 * 27 :, :] = jnp.zeros((SLOT, 128), F32)
+    round_wait(0)
+    round_signal(1)
     own_planes(xm, xs)
     for k in range(8):
         gt[:, 128 * k : 128 * k + 128] = gmb[2 * k : 2 * k + 2].reshape(128, 128).T
     kernel_grad(1)
     core_send(0)
-    round_wait(0)
-    round_signal(1)
+    round_wait(1)
+    round_signal(2)
     for side in range(2):
         halos[side][0].wait()
         halos[side][1].wait()
     rim_planes(halo_x, xs)
     kernel_grad(0)
     core_send(1)
-    round_wait(1)
-    round_signal(2)
+    round_wait(2)
+    xy_send(0)
     kernel_grad(2)
     core_send(2)
-    round_wait(2)
-    xy_send(0)
     xy_send(1)
+    own_planes(gm, gs)
     loads[3].wait()
-    products(xs, wv, 0, resp_hbm, 0, 1)
+    products(xs, wv, resp_ref, 0, 1)
     xy_send(2)
-    own_planes(gm, gs)
     halos[0][2].wait()
     halos[1][2].wait()
     rim_planes(halo_g, gs)
     transposed_weights()
-    products(xs, wv, 0, resp_hbm, 1, 4)
-    out_copy(0).start()
+    products(xs, wv, resp_ref, 1, 3)
     z_send(0)
     z_send(1)
     z_send(2)
-    products(gs, wt, 1, gin_hbm, 0, 3)
+    products(xs, wv, resp_ref, 3, 4)
+    products(gs, wt, gin_ref, 0, 3)
 
     def z_done(k, carry):
         source = lax.rem(me_z + k, 8)
@@ -421,16 +421,24 @@
 
     for k in range(1, 4):
         y_copy(me_y, k).start()
-    products(gs, wt, 1, gin_hbm, 3, 4)
-    out_copy(1).start()
+    products(gs, wt, gin_ref, 3, 4)
     for k in range(1, 4):
         y_copy(lax.rem(me_y + k, 4), k).wait_recv()
         y_copy(me_y, k).wait_send()
     for q in range(4):
         rows = min(PART, ROWS - PART * q)
         gw_ref[PART * q : PART * q + rows, :] = fin[q, :rows]
-    out_copy(0).wait()
-    out_copy(1).wait()
+
+
+def store_kernel(a, b, c, a_out, b_out, c_out, sem):
+    copies = [
+        pltpu.make_async_copy(src, dst, sem.at[i])
+        for i, (src, dst) in enumerate(((a, a_out), (b, b_out), (c, c_out)))
+    ]
+    for copy in copies:
+        copy.start()
+    for copy in copies:
+        copy.wait()
 
 
 def per_device(features, occupancy, neighbours, weight, cotangent):
@@ -439,9 +447,9 @@
     resp, gin, gw = pl.pallas_call(
         kernel,
         out_shape=(
-            jax.ShapeDtypeStruct((16, 64, 128), BF),
-            jax.ShapeDtypeStruct((16, 64, 128), BF),
-            jax.ShapeDtypeStruct((ROWS, 128), F32),
+            pltpu.VMEM((16, 64, 128), BF),
+            pltpu.VMEM((16, 64, 128), BF),
+            pltpu.VMEM((ROWS, 128), F32),
         ),
         in_specs=[
             anywhere,
@@ -450,7 +458,7 @@
             pl.BlockSpec(memory_space=pltpu.SMEM),
             anywhere,
         ],
-        out_specs=(anywhere, anywhere, pl.BlockSpec(memory_space=pltpu.VMEM)),
+        out_specs=(pl.BlockSpec(memory_space=pltpu.VMEM),) * 3,
         scratch_shapes=[
             pltpu.VMEM((2, 8, 64, 128), BF),
             pltpu.VMEM((2, 8, 64, 128), BF),
@@ -476,9 +484,7 @@
             pltpu.VMEM((8, SLOT, 128), F32),
             pltpu.VMEM((8, SLOT, 128), F32),
             pltpu.VMEM((4, SLOT, 128), F32),
-            pltpu.VMEM((2, 16, 64, 128), BF),
             dma((4,)),
-            dma((2,)),
             dma((3, 2)),
             dma((3, 2)),
             dma((3,)),
@@ -500,6 +506,15 @@
         neighbours[0],
         weight,
     )
+    in_vmem = pl.BlockSpec(memory_space=pltpu.VMEM)
+    resp, gin, gw = pl.pallas_call(
+        store_kernel,
+        out_shape=tuple(jax.ShapeDtypeStruct(v.shape, v.dtype) for v in (resp, gin, gw)),
+        in_specs=[in_vmem] * 3,
+        out_specs=(anywhere,) * 3,
+        scratch_shapes=[dma((3,))],
+        name="store_results",
+    )(*(pltpu.with_memory_space_constraint(v, pltpu.VMEM) for v in (resp, gin, gw)))
     shape = features.shape
     return resp.reshape(shape), gin.reshape(shape), gw
 

time: 36.6 us -> 32.5 us (0.89)
  local copies, waits for them, and re-layouts: 3.07 us -> 0 us
  Pallas kernels: 32.6 us -> 31.7 us
    unnamed x7 -> x0, local copies, waits for them, and re-layouts: 3.07 us -> none
    pallas_call x1 -> x2, Pallas kernels: 32.6 us -> 31.7 us  [the longest x1 30.9 us: per_device(): pl.pallas_call(kernel, out_shape=(pltpu.VMEM((16, 64, 128), BF), pltpu.VM...]
where the time goes in v4:
time: 32.5 us; the launch traced here: 32.3 us
  Pallas kernels  31.7 us (98%)
  between operations  0.64 us (2%)
    pallas_call x1, Pallas kernels, per_device(): pl.pallas_call(kernel, out_shape=(pltpu.VMEM((16, 64, 128), BF), pltpu.VM...  30.9 us
    pallas_call x1, Pallas kernels, per_device(): pl.pallas_call(store_kernel, out_shape=tuple((jax.ShapeDtypeStruct(v.shap...  0.82 us

profile of v4, /device:TPU:1, one launch (start us, length us, event | category | flops | bytes accessed | tf_op | source)
XLA Modules:
  0.0 32.3 jit_solution(7601330091291024583)
XLA Ops:
  0.6 30.9 %sparse_conv_step.1 = (bf16[16,64,128]{2,1,0:T(8,128)(2,1)S(1)}, bf16[16,64,128]{2,1,0:T(8,128)(2,1)S(1)}, f32[54,128]{1,0:T(8,128)S(1)}) custom-call(bf16[2,8,64,128]{3,2,1,0:T(8,128)(2,1)} %bitcast.6, bf16[2,8,64,128]{3,2,1,0:T(8,128)(2,1)} %bitcast.7, s32[2,8,8,8]{3,2,1,0:T(8,128)} %bitcast.8, s32[2,26]{1,0:T(2,128)} %bitcast.9, bf16[27,128,128]{2,1,0:T(8,128)(2,1)} %w_hbm.1), custom_call_target="tpu_custom_call" | custom-call | tf_op jit(solution)/shard_map/sparse_conv_step/pallas_call | solution.py:447
  31.5 0.8 %store_results.1 = (bf16[16,64,128]{2,1,0:T(8,128)(2,1)}, bf16[16,64,128]{2,1,0:T(8,128)(2,1)}, f32[54,128]{1,0:T(8,128)}) custom-call(bf16[16,64,128]{2,1,0:T(8,128)(2,1)S(1)} %get-tuple-element.9.a, bf16[16,64,128]{2,1,0:T(8,128)(2,1)S(1)} %get-tuple-element.10.b, f32[54,128]{1,0:T(8,128)S(1)} %get-tuple-element.11.c), custom_call_target="tpu_custom_call" | custom-call | tf_op jit(solution)/shard_map/store_results/pallas_call | solution.py:510

commit v5 on v4

--- a/solution.py
+++ b/solution.py
@@ -76,6 +76,34 @@
 
     def round_wait(r):
         pl.semaphore_wait(ready.at[r], 6)
+
+    for load in loads[:3]:
+        load.wait()
+
+    eye = (
+        lax.broadcasted_iota(jnp.int32, (8, 8, 8), 1)
+        == lax.broadcasted_iota(jnp.int32, (8, 8, 8), 2)
+    )
+    ones = jnp.ones((8, 128), F32)
+
+    def mask_of(occ):
+        spread = jnp.broadcast_to(occ[:, None, :], (8, 8, 8))
+        picked = jnp.where(eye & (spread > 0), 1.0, 0.0).astype(F32).reshape(64, 8)
+        return jnp.dot(picked, ones, preferred_element_type=F32)
+
+    def mask_plane(i, carry):
+        b, p = i // 8, lax.rem(i, 8)
+        m = mask_of(occv[b, p])
+        mask[i] = m
+        keep = m > 0.5
+        xk = jnp.where(keep, xv[b, p].astype(F32), 0.0)
+        gk = jnp.where(keep, gv[b, p].astype(F32), 0.0)
+        xm[i] = xk.reshape(8, 8, 128)
+        gm[i] = gk.reshape(8, 8, 128)
+        gmb[i] = gk.astype(BF)
+        return carry
+
+    lax.fori_loop(0, 16, mask_plane, 0, unroll=4)
 
     pl.semaphore_wait(barrier, 9)
 
@@ -101,33 +129,6 @@
             halos[side][t].start()
     round_signal(0)
 
-    for load in loads[:3]:
-        load.wait()
-
-    eye = (
-        lax.broadcasted_iota(jnp.int32, (8, 8, 8), 1)
-        == lax.broadcasted_iota(jnp.int32, (8, 8, 8), 2)
-    )
-    ones = jnp.ones((8, 128), F32)
-
-    def mask_of(occ):
-        spread = jnp.broadcast_to(occ[:, None, :], (8, 8, 8))
-        picked = jnp.where(eye & (spread > 0), 1.0, 0.0).astype(F32).reshape(64, 8)
-        return jnp.dot(picked, ones, preferred_element_type=F32)
-
-    def mask_plane(i, carry):
-        b, p = i // 8, lax.rem(i, 8)
-        m = mask_of(occv[b, p])
-        mask[i] = m
-        keep = m > 0.5
-        xk = jnp.where(keep, xv[b, p].astype(F32), 0.0)
-        gk = jnp.where(keep, gv[b, p].astype(F32), 0.0)
-        xm[i] = xk.reshape(8, 8, 128)
-        gm[i] = gk.reshape(8, 8, 128)
-        gmb[i] = gk.astype(BF)
-        return carry
-
-    lax.fori_loop(0, 16, mask_plane, 0, unroll=4)
 
     zi = lax.broadcasted_iota(jnp.int32, (10, 8, 128), 1)
 
@@ -331,12 +332,12 @@
 
         lax.fori_loop(z0, z0 + nz, send, 0)
 
-    def transposed_weights():
+    def transposed_weights(lo, hi):
         def turn(t, carry):
             wt[26 - t] = wv[t].T
             return carry
 
-        lax.fori_loop(0, 27, turn, 0)
+        lax.fori_loop(lo, hi, turn, 0, unroll=3)
 
     def product(shifts, taps, out, part):
         b = part // 2
@@ -370,6 +371,8 @@
     core_send(0)
     round_wait(1)
     round_signal(2)
+    loads[3].wait()
+    transposed_weights(0, 9)
     for side in range(2):
         halos[side][0].wait()
         halos[side][1].wait()
@@ -382,19 +385,18 @@
     core_send(2)
     xy_send(1)
     own_planes(gm, gs)
-    loads[3].wait()
     products(xs, wv, resp_ref, 0, 1)
     xy_send(2)
     halos[0][2].wait()
     halos[1][2].wait()
     rim_planes(halo_g, gs)
-    transposed_weights()
+    transposed_weights(9, 27)
     products(xs, wv, resp_ref, 1, 3)
     z_send(0)
     z_send(1)
     z_send(2)
     products(xs, wv, resp_ref, 3, 4)
-    products(gs, wt, gin_ref, 0, 3)
+    products(gs, wt, gin_ref, 0, 2)
 
     def z_done(k, carry):
         source = lax.rem(me_z + k, 8)
@@ -421,7 +423,7 @@
 
     for k in range(1, 4):
         y_copy(me_y, k).start()
-    products(gs, wt, gin_ref, 3, 4)
+    products(gs, wt, gin_ref, 2, 4)
     for k in range(1, 4):
         y_copy(lax.rem(me_y + k, 4), k).wait_recv()
         y_copy(me_y, k).wait_send()

time: 32.5 us -> 32.4 us (level)
  the two profiles are of different devices: /device:TPU:1 before, /device:TPU:8 now
where the time goes in v5:
time: 32.4 us; the launch traced here: 32.3 us
  Pallas kernels  31.6 us (98%)
  between operations  0.64 us (2%)
    pallas_call x1, Pallas kernels, per_device(): pl.pallas_call(kernel, out_shape=(pltpu.VMEM((16, 64, 128), BF), pltpu.VM...  30.8 us
    pallas_call x1, Pallas kernels, per_device(): pl.pallas_call(store_kernel, out_shape=tuple((jax.ShapeDtypeStruct(v.shap...  0.82 us

profile of v5, /device:TPU:8, one launch (start us, length us, event | category | flops | bytes accessed | tf_op | source)
XLA Modules:
  0.0 32.3 jit_solution(10879081325873288202)
XLA Ops:
  0.6 30.8 %sparse_conv_step.1 = (bf16[16,64,128]{2,1,0:T(8,128)(2,1)S(1)}, bf16[16,64,128]{2,1,0:T(8,128)(2,1)S(1)}, f32[54,128]{1,0:T(8,128)S(1)}) custom-call(bf16[2,8,64,128]{3,2,1,0:T(8,128)(2,1)} %bitcast.6, bf16[2,8,64,128]{3,2,1,0:T(8,128)(2,1)} %bitcast.7, s32[2,8,8,8]{3,2,1,0:T(8,128)} %bitcast.8, s32[2,26]{1,0:T(2,128)} %bitcast.9, bf16[27,128,128]{2,1,0:T(8,128)(2,1)} %w_hbm.1), custom_call_target="tpu_custom_call" | custom-call | tf_op jit(solution)/shard_map/sparse_conv_step/pallas_call | solution.py:449
  31.4 0.8 %store_results.1 = (bf16[16,64,128]{2,1,0:T(8,128)(2,1)}, bf16[16,64,128]{2,1,0:T(8,128)(2,1)}, f32[54,128]{1,0:T(8,128)}) custom-call(bf16[16,64,128]{2,1,0:T(8,128)(2,1)S(1)} %get-tuple-element.9.a, bf16[16,64,128]{2,1,0:T(8,128)(2,1)S(1)} %get-tuple-element.10.b, f32[54,128]{1,0:T(8,128)S(1)} %get-tuple-element.11.c), custom_call_target="tpu_custom_call" | custom-call | tf_op jit(solution)/shard_map/store_results/pallas_call | solution.py:512
